TPU v7x, 32 devices: a whole 2x2x4 slice. The times are simulated.
32 devices in a mesh: layer: 8 (over z, x), lat: 4 (over y, core).
Axes of the slice: x: 2, y: 2, z: 4, core: 2. Of those that a mesh axis runs over, the one named last changes fastest.
Arguments:
- inverse: bfloat16 [8, 8, 512, 512], P('layer', 'lat')
- tiles: bfloat16 [1024, 256], P(('layer', 'lat')), may hold values from -6 to 6
- tile_dest: int32 [1024, 1], P(('layer', 'lat')), may hold values from 0 to 31; in each aligned block of 32 rows (0 to 31, 32 to 63, ...) at most 2 rows name the same one
- tile_code: int32 [1024], P(('layer', 'lat')), may hold values from 0 to 31
Outputs:
- solution: float32 [8, 8, 8, 512], P('layer', 'lat')
Inputs may be any that keep to these rules, and one draw needn't show every extreme that they name: `tile_dest`: the rows of one device name any one device at most 2 times; in every draw some device's rows name some device exactly 2 times.
All inputs are finite; a program needn't handle non-finite values.
Results may differ from a plain program's by a relative error of at most 0.004.
Values may be sent and summed in bfloat16 or wider, within the bound.
A program may use at most 128 MiB of HBM per device.

v0:
```python
import jax
import jax.numpy as jnp
from jax import lax
from jax.sharding import PartitionSpec as P

SRC = 8
CAP = 2


def from_behind(block, axis, distance):
    devices = range(lax.axis_size(axis))
    route = [(i - distance, i) for i in devices if i - distance in devices]
    return lax.ppermute(block, axis, route)


def apply_block(matrix, vectors):
    return jnp.einsum("bij,bsj->bsi", matrix, vectors, precision=lax.Precision.HIGHEST)


def body(inverse, tiles, tile_dest, tile_code):
    layers = lax.axis_size("layer")
    lateral = lax.axis_size("lat")
    devices = layers * lateral
    inverses = inverse[0]
    blocks = inverses.shape[0]
    size_m = inverses.shape[1]
    trace_len = tiles.shape[1]
    planes = size_m // trace_len
    far_rows = trace_len * (planes - 1)
    target = tile_dest[:, 0]
    matches = (target[:, None] == jnp.arange(devices, dtype=jnp.int32)[None, :]).astype(jnp.int32)
    order_at = jnp.sum((jnp.cumsum(matches, axis=0) - matches) * matches, axis=1)
    slot_at = target * CAP + order_at
    send_tiles = jnp.zeros((devices * CAP, trace_len), jnp.bfloat16).at[slot_at].set(tiles)
    send_tiles = send_tiles.reshape(layers, lateral, CAP, trace_len)
    send_codes = jnp.full((devices * CAP,), -1, jnp.int32).at[slot_at].set(tile_code)
    send_codes = send_codes.reshape(layers, lateral, CAP)
    got_tiles, got_codes = (
        lax.all_to_all(
            lax.all_to_all(send_tiles, "layer", split_axis=0, concat_axis=0, tiled=True),
            "lat",
            split_axis=1,
            concat_axis=1,
            tiled=True,
        ),
        lax.all_to_all(
            lax.all_to_all(send_codes, "layer", split_axis=0, concat_axis=0, tiled=True),
            "lat",
            split_axis=1,
            concat_axis=1,
            tiled=True,
        ),
    )
    codes_all = SRC * planes * blocks
    table = (jnp.arange(codes_all, dtype=jnp.int32)[:, None] == got_codes.reshape(1, -1)).astype(
        jnp.bfloat16
    )
    summed = jnp.dot(table, got_tiles.reshape(-1, trace_len), preferred_element_type=jnp.float32)
    summed = (
        summed.reshape(SRC, planes, blocks, trace_len)
        .transpose(2, 0, 1, 3)
        .reshape(blocks, SRC, size_m)
    )
    source_field = summed.astype(jnp.bfloat16)
    local_solve = jnp.einsum(
        "bij,bsj->bsi", inverses, source_field, preferred_element_type=jnp.float32
    )
    down_matrix = inverses[:, far_rows:, :trace_len].astype(jnp.float32)
    up_matrix = inverses[:, :trace_len, far_rows:].astype(jnp.float32)
    down_offset = local_solve[:, :, far_rows:]
    up_offset = local_solve[:, :, :trace_len]
    empty = jnp.zeros_like(up_offset)

    def down_turn(turn, state_now):
        incoming = from_behind(state_now[1], "layer", 1)
        return (incoming, apply_block(down_matrix, incoming) + down_offset)

    def up_turn(turn, state_now):
        incoming = from_behind(state_now[1], "layer", -1)
        return (incoming, apply_block(up_matrix, incoming) + up_offset)

    from_above = lax.fori_loop(0, layers, down_turn, (empty, empty))[0]
    from_below = lax.fori_loop(0, layers, up_turn, (empty, empty))[0]
    above_trace = from_above.astype(jnp.bfloat16)
    below_trace = from_below.astype(jnp.bfloat16)
    solution = local_solve + jnp.einsum(
        "bij,bsj->bsi", inverses[:, :, :trace_len], above_trace, preferred_element_type=jnp.float32
    )
    solution = solution + jnp.einsum(
        "bij,bsj->bsi", inverses[:, :, far_rows:], below_trace, preferred_element_type=jnp.float32
    )
    return solution[None]


def solution(mesh):
    in_specs = (
        P("layer", "lat", None, None),
        P(("layer", "lat"), None),
        P(("layer", "lat"), None),
        P(("layer", "lat")),
    )
    out_specs = P("layer", "lat", None, None)
    return jax.shard_map(body, mesh=mesh, in_specs=in_specs, out_specs=out_specs, check_vma=False)
```

profile of v0, /device:TPU:0, one launch (start us, length us, event | category | flops | bytes accessed | tf_op | source)
XLA Modules:
  0.0 155.0 jit_solution(9928905523274800462)
XLA Ops:
  2.6 7.3 %all-to-all-start = ((s32[8,4,2]{1,2,0:T(2,128)}), s32[8,4,2]{1,2,0:T(2,128)S(1)}, u32[]{:S(2)}, u32[]{:S(2)}) async-start(s32[8,4,2]{1,2,0:T(2,128)} %copy.12), calls=%async_computation | async-start | bytes 16384 | tf_op jit(solution)/shard_map/all_to_all | solution.py:47
  11.4 5.0 %all-to-all-done = s32[8,4,2]{1,2,0:T(2,128)S(1)} async-done(((s32[8,4,2]{1,2,0:T(2,128)}), s32[8,4,2]{1,2,0:T(2,128)S(1)}, u32[]{:S(2)}, u32[]{:S(2)}) %all-to-all-start) | async-done | bytes 288 | tf_op jit(solution)/shard_map/all_to_all | solution.py:47
  16.4 3.3 %all-to-all-start.2 = ((bf16[8,4,2,256]{3,2,1,0:T(2,128)(2,1)}), bf16[8,4,2,256]{3,2,1,0:T(2,128)(2,1)S(1)}, u32[]{:S(2)}, u32[]{:S(2)}) async-start(bf16[8,4,2,256]{3,2,1,0:T(2,128)(2,1)} %reshape.38), calls=%async_computation.2 | async-start | bytes 65536 | tf_op jit(solution)/shard_map/all_to_all | solution.py:40
  20.4 5.9 %all-to-all-done.2 = bf16[8,4,2,256]{3,2,1,0:T(2,128)(2,1)S(1)} async-done(((bf16[8,4,2,256]{3,2,1,0:T(2,128)(2,1)}), bf16[8,4,2,256]{3,2,1,0:T(2,128)(2,1)S(1)}, u32[]{:S(2)}, u32[]{:S(2)}) %all-to-all-start.2) | async-done | bytes 32800 | tf_op jit(solution)/shard_map/all_to_all | solution.py:40
  26.4 3.2 %all-to-all-start.1 = ((s32[8,4,2]{0,2,1:T(2,128)}), s32[8,4,2]{0,2,1:T(2,128)S(1)}, u32[]{:S(2)}, u32[]{:S(2)}) async-start(s32[8,4,2]{0,2,1:T(2,128)} %copy.13), calls=%async_computation.1 | async-start | bytes 8192 | tf_op jit(solution)/shard_map/all_to_all | solution.py:46
  33.4 3.3 %all-to-all-start.3 = ((bf16[8,4,2,256]{3,2,0,1:T(2,128)(2,1)}), bf16[8,4,2,256]{3,2,0,1:T(2,128)(2,1)S(1)}, u32[]{:S(2)}, u32[]{:S(2)}) async-start(bf16[8,4,2,256]{3,2,0,1:T(2,128)(2,1)} %copy.15), calls=%async_computation.3 | async-start | bytes 65536 | tf_op jit(solution)/shard_map/all_to_all | solution.py:39
  36.9 3.7 %all-to-all-done.3 = bf16[8,4,2,256]{3,2,0,1:T(2,128)(2,1)S(1)} async-done(((bf16[8,4,2,256]{3,2,0,1:T(2,128)(2,1)}), bf16[8,4,2,256]{3,2,0,1:T(2,128)(2,1)S(1)}, u32[]{:S(2)}, u32[]{:S(2)}) %all-to-all-start.3) | async-done | bytes 32800 | tf_op jit(solution)/shard_map/all_to_all | solution.py:39
  41.8 52.5 %while.26 = (s32[]{:T(128)}, f32[2,8,256]{2,1,0:T(8,128)}, f32[2,8,256]{2,1,0:T(8,128)S(1)}, f32[2,256,256]{2,1,0:T(8,128)S(1)}, f32[2,8,256]{2,1,0:T(8,128)S(1)}, /*index=5*/s32[]{:T(128)}, s32[]{:T(128)}) while((s32[]{:T(128)}, f32[2,8,256]{2,1,0:T(8,128)}, f32[2,8,256]{2,1,0:T(8,128)S(1)}, f32[2,256,256]{2,1,0:T(8,128)S(1)}, ...), condition=%wide.region_5.6_spmd.clone, body=%wide.region_4.5_spmd.clone.sunk | while | flops 12591107 | bytes 737435 | solution.py:82
  46.2 4.2 %collective-permute-start = (f32[2,8,256]{2,1,0:T(8,128)S(1)}, f32[2,8,256]{2,1,0:T(8,128)S(1)}, u32[]{:S(2)}, u32[]{:S(2)}) collective-permute-start(f32[2,8,256]{2,1,0:T(8,128)S(1)} %broadcast_select_fusion.4), channel_id=1, source_target_pairs={{0,4},{4,8},{8,12},{12,16},{16,20},{20,24},{24,28},{1,5},{5,9},{9,... | collective-permute-start | bytes 49160 | tf_op jit(solution)/shard_map/while/body/eval_jaxpr/ppermute | solution.py:13
  52.5 4.2 %collective-permute-start = (f32[2,8,256]{2,1,0:T(8,128)S(1)}, f32[2,8,256]{2,1,0:T(8,128)S(1)}, u32[]{:S(2)}, u32[]{:S(2)}) collective-permute-start(f32[2,8,256]{2,1,0:T(8,128)S(1)} %broadcast_select_fusion.4), channel_id=1, source_target_pairs={{0,4},{4,8},{8,12},{12,16},{16,20},{20,24},{24,28},{1,5},{5,9},{9,... | collective-permute-start | bytes 49160 | tf_op jit(solution)/shard_map/while/body/eval_jaxpr/ppermute | solution.py:13
  58.7 5.1 %collective-permute-start = (f32[2,8,256]{2,1,0:T(8,128)S(1)}, f32[2,8,256]{2,1,0:T(8,128)S(1)}, u32[]{:S(2)}, u32[]{:S(2)}) collective-permute-start(f32[2,8,256]{2,1,0:T(8,128)S(1)} %broadcast_select_fusion.4), channel_id=1, source_target_pairs={{0,4},{4,8},{8,12},{12,16},{16,20},{20,24},{24,28},{1,5},{5,9},{9,... | collective-permute-start | bytes 49160 | tf_op jit(solution)/shard_map/while/body/eval_jaxpr/ppermute | solution.py:13
  65.8 5.1 %collective-permute-start = (f32[2,8,256]{2,1,0:T(8,128)S(1)}, f32[2,8,256]{2,1,0:T(8,128)S(1)}, u32[]{:S(2)}, u32[]{:S(2)}) collective-permute-start(f32[2,8,256]{2,1,0:T(8,128)S(1)} %broadcast_select_fusion.4), channel_id=1, source_target_pairs={{0,4},{4,8},{8,12},{12,16},{16,20},{20,24},{24,28},{1,5},{5,9},{9,... | collective-permute-start | bytes 49160 | tf_op jit(solution)/shard_map/while/body/eval_jaxpr/ppermute | solution.py:13
  72.9 5.1 %collective-permute-start = (f32[2,8,256]{2,1,0:T(8,128)S(1)}, f32[2,8,256]{2,1,0:T(8,128)S(1)}, u32[]{:S(2)}, u32[]{:S(2)}) collective-permute-start(f32[2,8,256]{2,1,0:T(8,128)S(1)} %broadcast_select_fusion.4), channel_id=1, source_target_pairs={{0,4},{4,8},{8,12},{12,16},{16,20},{20,24},{24,28},{1,5},{5,9},{9,... | collective-permute-start | bytes 49160 | tf_op jit(solution)/shard_map/while/body/eval_jaxpr/ppermute | solution.py:13
  80.1 5.1 %collective-permute-start = (f32[2,8,256]{2,1,0:T(8,128)S(1)}, f32[2,8,256]{2,1,0:T(8,128)S(1)}, u32[]{:S(2)}, u32[]{:S(2)}) collective-permute-start(f32[2,8,256]{2,1,0:T(8,128)S(1)} %broadcast_select_fusion.4), channel_id=1, source_target_pairs={{0,4},{4,8},{8,12},{12,16},{16,20},{20,24},{24,28},{1,5},{5,9},{9,... | collective-permute-start | bytes 49160 | tf_op jit(solution)/shard_map/while/body/eval_jaxpr/ppermute | solution.py:13
  87.2 5.1 %collective-permute-start = (f32[2,8,256]{2,1,0:T(8,128)S(1)}, f32[2,8,256]{2,1,0:T(8,128)S(1)}, u32[]{:S(2)}, u32[]{:S(2)}) collective-permute-start(f32[2,8,256]{2,1,0:T(8,128)S(1)} %broadcast_select_fusion.4), channel_id=1, source_target_pairs={{0,4},{4,8},{8,12},{12,16},{16,20},{20,24},{24,28},{1,5},{5,9},{9,... | collective-permute-start | bytes 49160 | tf_op jit(solution)/shard_map/while/body/eval_jaxpr/ppermute | solution.py:13
  95.9 57.5 %while.27 = (s32[]{:T(128)}, f32[2,8,256]{2,1,0:T(8,128)}, f32[2,8,256]{2,1,0:T(8,128)S(1)}, f32[2,256,256]{2,1,0:T(8,128)S(1)}, f32[2,8,256]{2,1,0:T(8,128)S(1)}, /*index=5*/s32[]{:T(128)}, s32[]{:T(128)}) while((s32[]{:T(128)}, f32[2,8,256]{2,1,0:T(8,128)}, f32[2,8,256]{2,1,0:T(8,128)S(1)}, f32[2,256,256]{2,1,0:T(8,128)S(1)}, ...), condition=%wide.region_7.8_spmd.clone, body=%wide.region_6.7_spmd.clone.sunk | while | flops 12591107 | bytes 737435 | solution.py:83
  97.2 5.5 %collective-permute-done.1 = f32[2,8,256]{2,1,0:T(8,128)S(1)} collective-permute-done((f32[2,8,256]{2,1,0:T(8,128)S(1)}, f32[2,8,256]{2,1,0:T(8,128)S(1)}, u32[]{:S(2)}, u32[]{:S(2)}) %collective-permute-start.1) | collective-permute-done | bytes 16416 | tf_op jit(solution)/shard_map/while/body/eval_jaxpr/ppermute | solution.py:13
  104.6 5.5 %collective-permute-done.1 = f32[2,8,256]{2,1,0:T(8,128)S(1)} collective-permute-done((f32[2,8,256]{2,1,0:T(8,128)S(1)}, f32[2,8,256]{2,1,0:T(8,128)S(1)}, u32[]{:S(2)}, u32[]{:S(2)}) %collective-permute-start.1) | collective-permute-done | bytes 16416 | tf_op jit(solution)/shard_map/while/body/eval_jaxpr/ppermute | solution.py:13
  112.0 5.3 %collective-permute-done.1 = f32[2,8,256]{2,1,0:T(8,128)S(1)} collective-permute-done((f32[2,8,256]{2,1,0:T(8,128)S(1)}, f32[2,8,256]{2,1,0:T(8,128)S(1)}, u32[]{:S(2)}, u32[]{:S(2)}) %collective-permute-start.1) | collective-permute-done | bytes 16416 | tf_op jit(solution)/shard_map/while/body/eval_jaxpr/ppermute | solution.py:13
  119.2 5.1 %collective-permute-done.1 = f32[2,8,256]{2,1,0:T(8,128)S(1)} collective-permute-done((f32[2,8,256]{2,1,0:T(8,128)S(1)}, f32[2,8,256]{2,1,0:T(8,128)S(1)}, u32[]{:S(2)}, u32[]{:S(2)}) %collective-permute-start.1) | collective-permute-done | bytes 16416 | tf_op jit(solution)/shard_map/while/body/eval_jaxpr/ppermute | solution.py:13
  126.2 5.2 %collective-permute-done.1 = f32[2,8,256]{2,1,0:T(8,128)S(1)} collective-permute-done((f32[2,8,256]{2,1,0:T(8,128)S(1)}, f32[2,8,256]{2,1,0:T(8,128)S(1)}, u32[]{:S(2)}, u32[]{:S(2)}) %collective-permute-start.1) | collective-permute-done | bytes 16416 | tf_op jit(solution)/shard_map/while/body/eval_jaxpr/ppermute | solution.py:13
  133.4 5.2 %collective-permute-done.1 = f32[2,8,256]{2,1,0:T(8,128)S(1)} collective-permute-done((f32[2,8,256]{2,1,0:T(8,128)S(1)}, f32[2,8,256]{2,1,0:T(8,128)S(1)}, u32[]{:S(2)}, u32[]{:S(2)}) %collective-permute-start.1) | collective-permute-done | bytes 16416 | tf_op jit(solution)/shard_map/while/body/eval_jaxpr/ppermute | solution.py:13
  140.5 5.2 %collective-permute-done.1 = f32[2,8,256]{2,1,0:T(8,128)S(1)} collective-permute-done((f32[2,8,256]{2,1,0:T(8,128)S(1)}, f32[2,8,256]{2,1,0:T(8,128)S(1)}, u32[]{:S(2)}, u32[]{:S(2)}) %collective-permute-start.1) | collective-permute-done | bytes 16416 | tf_op jit(solution)/shard_map/while/body/eval_jaxpr/ppermute | solution.py:13
  147.6 5.2 %collective-permute-done.1 = f32[2,8,256]{2,1,0:T(8,128)S(1)} collective-permute-done((f32[2,8,256]{2,1,0:T(8,128)S(1)}, f32[2,8,256]{2,1,0:T(8,128)S(1)}, u32[]{:S(2)}, u32[]{:S(2)}) %collective-permute-start.1) | collective-permute-done | bytes 16416 | tf_op jit(solution)/shard_map/while/body/eval_jaxpr/ppermute | solution.py:13
  (113 shorter events, 46.9 us)
Async XLA Ops:
  0.0 0.7 copy-start.3
  2.6 13.8 %all-to-all-start = ((s32[8,4,2]{1,2,0:T(2,128)}), s32[8,4,2]{1,2,0:T(2,128)S(1)}, u32[]{:S(2)}, u32[]{:S(2)}) async-start(s32[8,4,2]{1,2,0:T(2,128)} %copy.12), calls=%async_computation | async-start | bytes 16384 | tf_op jit(solution)/shard_map/all_to_all | solution.py:47
  11.4 29.4 %copy-start = (bf16[1,2,512,512]{3,2,1,0:T(8,128)(2,1)S(1)}, bf16[1,2,512,512]{3,2,1,0:T(8,128)(2,1)}, u32[]{:S(2)}) copy-start(bf16[1,2,512,512]{3,2,1,0:T(8,128)(2,1)} %param.8) | copy-start | bytes 3145732
  16.4 10.0 %all-to-all-start.2 = ((bf16[8,4,2,256]{3,2,1,0:T(2,128)(2,1)}), bf16[8,4,2,256]{3,2,1,0:T(2,128)(2,1)S(1)}, u32[]{:S(2)}, u32[]{:S(2)}) async-start(bf16[8,4,2,256]{3,2,1,0:T(2,128)(2,1)} %reshape.38), calls=%async_computation.2 | async-start | bytes 65536 | tf_op jit(solution)/shard_map/all_to_all | solution.py:40
  26.4 7.0 %all-to-all-start.1 = ((s32[8,4,2]{0,2,1:T(2,128)}), s32[8,4,2]{0,2,1:T(2,128)S(1)}, u32[]{:S(2)}, u32[]{:S(2)}) async-start(s32[8,4,2]{0,2,1:T(2,128)} %copy.13), calls=%async_computation.1 | async-start | bytes 8192 | tf_op jit(solution)/shard_map/all_to_all | solution.py:46
  33.4 7.2 %all-to-all-start.3 = ((bf16[8,4,2,256]{3,2,0,1:T(2,128)(2,1)}), bf16[8,4,2,256]{3,2,0,1:T(2,128)(2,1)S(1)}, u32[]{:S(2)}, u32[]{:S(2)}) async-start(bf16[8,4,2,256]{3,2,0,1:T(2,128)(2,1)} %copy.15), calls=%async_computation.3 | async-start | bytes 65536 | tf_op jit(solution)/shard_map/all_to_all | solution.py:39
  41.8 3.8 %collective-permute-start = (f32[2,8,256]{2,1,0:T(8,128)S(1)}, f32[2,8,256]{2,1,0:T(8,128)S(1)}, u32[]{:S(2)}, u32[]{:S(2)}) collective-permute-start(f32[2,8,256]{2,1,0:T(8,128)S(1)} %broadcast_select_fusion.4), channel_id=1, source_target_pairs={{0,4},{4,8},{8,12},{12,16},{16,20},{20,24},{24,28},{1,5},{5,9},{9,... | collective-permute-start | bytes 49160 | tf_op jit(solution)/shard_map/while/body/eval_jaxpr/ppermute | solution.py:13
  46.2 5.6 %collective-permute-start = (f32[2,8,256]{2,1,0:T(8,128)S(1)}, f32[2,8,256]{2,1,0:T(8,128)S(1)}, u32[]{:S(2)}, u32[]{:S(2)}) collective-permute-start(f32[2,8,256]{2,1,0:T(8,128)S(1)} %broadcast_select_fusion.4), channel_id=1, source_target_pairs={{0,4},{4,8},{8,12},{12,16},{16,20},{20,24},{24,28},{1,5},{5,9},{9,... | collective-permute-start | bytes 49160 | tf_op jit(solution)/shard_map/while/body/eval_jaxpr/ppermute | solution.py:13
  52.5 5.6 %collective-permute-start = (f32[2,8,256]{2,1,0:T(8,128)S(1)}, f32[2,8,256]{2,1,0:T(8,128)S(1)}, u32[]{:S(2)}, u32[]{:S(2)}) collective-permute-start(f32[2,8,256]{2,1,0:T(8,128)S(1)} %broadcast_select_fusion.4), channel_id=1, source_target_pairs={{0,4},{4,8},{8,12},{12,16},{16,20},{20,24},{24,28},{1,5},{5,9},{9,... | collective-permute-start | bytes 49160 | tf_op jit(solution)/shard_map/while/body/eval_jaxpr/ppermute | solution.py:13
  58.1 0.6 copy-start.2
  58.7 6.5 %collective-permute-start = (f32[2,8,256]{2,1,0:T(8,128)S(1)}, f32[2,8,256]{2,1,0:T(8,128)S(1)}, u32[]{:S(2)}, u32[]{:S(2)}) collective-permute-start(f32[2,8,256]{2,1,0:T(8,128)S(1)} %broadcast_select_fusion.4), channel_id=1, source_target_pairs={{0,4},{4,8},{8,12},{12,16},{16,20},{20,24},{24,28},{1,5},{5,9},{9,... | collective-permute-start | bytes 49160 | tf_op jit(solution)/shard_map/while/body/eval_jaxpr/ppermute | solution.py:13
  65.2 0.6 copy-start.2
  65.8 6.5 %collective-permute-start = (f32[2,8,256]{2,1,0:T(8,128)S(1)}, f32[2,8,256]{2,1,0:T(8,128)S(1)}, u32[]{:S(2)}, u32[]{:S(2)}) collective-permute-start(f32[2,8,256]{2,1,0:T(8,128)S(1)} %broadcast_select_fusion.4), channel_id=1, source_target_pairs={{0,4},{4,8},{8,12},{12,16},{16,20},{20,24},{24,28},{1,5},{5,9},{9,... | collective-permute-start | bytes 49160 | tf_op jit(solution)/shard_map/while/body/eval_jaxpr/ppermute | solution.py:13
  72.9 6.5 %collective-permute-start = (f32[2,8,256]{2,1,0:T(8,128)S(1)}, f32[2,8,256]{2,1,0:T(8,128)S(1)}, u32[]{:S(2)}, u32[]{:S(2)}) collective-permute-start(f32[2,8,256]{2,1,0:T(8,128)S(1)} %broadcast_select_fusion.4), channel_id=1, source_target_pairs={{0,4},{4,8},{8,12},{12,16},{16,20},{20,24},{24,28},{1,5},{5,9},{9,... | collective-permute-start | bytes 49160 | tf_op jit(solution)/shard_map/while/body/eval_jaxpr/ppermute | solution.py:13
  80.1 6.5 %collective-permute-start = (f32[2,8,256]{2,1,0:T(8,128)S(1)}, f32[2,8,256]{2,1,0:T(8,128)S(1)}, u32[]{:S(2)}, u32[]{:S(2)}) collective-permute-start(f32[2,8,256]{2,1,0:T(8,128)S(1)} %broadcast_select_fusion.4), channel_id=1, source_target_pairs={{0,4},{4,8},{8,12},{12,16},{16,20},{20,24},{24,28},{1,5},{5,9},{9,... | collective-permute-start | bytes 49160 | tf_op jit(solution)/shard_map/while/body/eval_jaxpr/ppermute | solution.py:13
  87.2 6.5 %collective-permute-start = (f32[2,8,256]{2,1,0:T(8,128)S(1)}, f32[2,8,256]{2,1,0:T(8,128)S(1)}, u32[]{:S(2)}, u32[]{:S(2)}) collective-permute-start(f32[2,8,256]{2,1,0:T(8,128)S(1)} %broadcast_select_fusion.4), channel_id=1, source_target_pairs={{0,4},{4,8},{8,12},{12,16},{16,20},{20,24},{24,28},{1,5},{5,9},{9,... | collective-permute-start | bytes 49160 | tf_op jit(solution)/shard_map/while/body/eval_jaxpr/ppermute | solution.py:13
  95.9 6.8 %collective-permute-start.1 = (f32[2,8,256]{2,1,0:T(8,128)S(1)}, f32[2,8,256]{2,1,0:T(8,128)S(1)}, u32[]{:S(2)}, u32[]{:S(2)}) collective-permute-start(f32[2,8,256]{2,1,0:T(8,128)S(1)} %broadcast_select_fusion.5), channel_id=1, source_target_pairs={{4,0},{8,4},{12,8},{16,12},{20,16},{24,20},{28,24},{5,1},{9,5},{13... | collective-permute-start | bytes 49160 | tf_op jit(solution)/shard_map/while/body/eval_jaxpr/ppermute | solution.py:13
  103.3 6.8 %collective-permute-start.1 = (f32[2,8,256]{2,1,0:T(8,128)S(1)}, f32[2,8,256]{2,1,0:T(8,128)S(1)}, u32[]{:S(2)}, u32[]{:S(2)}) collective-permute-start(f32[2,8,256]{2,1,0:T(8,128)S(1)} %broadcast_select_fusion.5), channel_id=1, source_target_pairs={{4,0},{8,4},{12,8},{16,12},{20,16},{24,20},{28,24},{5,1},{9,5},{13... | collective-permute-start | bytes 49160 | tf_op jit(solution)/shard_map/while/body/eval_jaxpr/ppermute | solution.py:13
  110.7 6.6 %collective-permute-start.1 = (f32[2,8,256]{2,1,0:T(8,128)S(1)}, f32[2,8,256]{2,1,0:T(8,128)S(1)}, u32[]{:S(2)}, u32[]{:S(2)}) collective-permute-start(f32[2,8,256]{2,1,0:T(8,128)S(1)} %broadcast_select_fusion.5), channel_id=1, source_target_pairs={{4,0},{8,4},{12,8},{16,12},{20,16},{24,20},{28,24},{5,1},{9,5},{13... | collective-permute-start | bytes 49160 | tf_op jit(solution)/shard_map/while/body/eval_jaxpr/ppermute | solution.py:13
  117.9 6.4 %collective-permute-start.1 = (f32[2,8,256]{2,1,0:T(8,128)S(1)}, f32[2,8,256]{2,1,0:T(8,128)S(1)}, u32[]{:S(2)}, u32[]{:S(2)}) collective-permute-start(f32[2,8,256]{2,1,0:T(8,128)S(1)} %broadcast_select_fusion.5), channel_id=1, source_target_pairs={{4,0},{8,4},{12,8},{16,12},{20,16},{24,20},{28,24},{5,1},{9,5},{13... | collective-permute-start | bytes 49160 | tf_op jit(solution)/shard_map/while/body/eval_jaxpr/ppermute | solution.py:13
  125.0 6.5 %collective-permute-start.1 = (f32[2,8,256]{2,1,0:T(8,128)S(1)}, f32[2,8,256]{2,1,0:T(8,128)S(1)}, u32[]{:S(2)}, u32[]{:S(2)}) collective-permute-start(f32[2,8,256]{2,1,0:T(8,128)S(1)} %broadcast_select_fusion.5), channel_id=1, source_target_pairs={{4,0},{8,4},{12,8},{16,12},{20,16},{24,20},{28,24},{5,1},{9,5},{13... | collective-permute-start | bytes 49160 | tf_op jit(solution)/shard_map/while/body/eval_jaxpr/ppermute | solution.py:13
  132.1 6.5 %collective-permute-start.1 = (f32[2,8,256]{2,1,0:T(8,128)S(1)}, f32[2,8,256]{2,1,0:T(8,128)S(1)}, u32[]{:S(2)}, u32[]{:S(2)}) collective-permute-start(f32[2,8,256]{2,1,0:T(8,128)S(1)} %broadcast_select_fusion.5), channel_id=1, source_target_pairs={{4,0},{8,4},{12,8},{16,12},{20,16},{24,20},{28,24},{5,1},{9,5},{13... | collective-permute-start | bytes 49160 | tf_op jit(solution)/shard_map/while/body/eval_jaxpr/ppermute | solution.py:13
  139.2 6.5 %collective-permute-start.1 = (f32[2,8,256]{2,1,0:T(8,128)S(1)}, f32[2,8,256]{2,1,0:T(8,128)S(1)}, u32[]{:S(2)}, u32[]{:S(2)}) collective-permute-start(f32[2,8,256]{2,1,0:T(8,128)S(1)} %broadcast_select_fusion.5), channel_id=1, source_target_pairs={{4,0},{8,4},{12,8},{16,12},{20,16},{24,20},{28,24},{5,1},{9,5},{13... | collective-permute-start | bytes 49160 | tf_op jit(solution)/shard_map/while/body/eval_jaxpr/ppermute | solution.py:13
  146.3 6.5 %collective-permute-start.1 = (f32[2,8,256]{2,1,0:T(8,128)S(1)}, f32[2,8,256]{2,1,0:T(8,128)S(1)}, u32[]{:S(2)}, u32[]{:S(2)}) collective-permute-start(f32[2,8,256]{2,1,0:T(8,128)S(1)} %broadcast_select_fusion.5), channel_id=1, source_target_pairs={{4,0},{8,4},{12,8},{16,12},{20,16},{24,20},{28,24},{5,1},{9,5},{13... | collective-permute-start | bytes 49160 | tf_op jit(solution)/shard_map/while/body/eval_jaxpr/ppermute | solution.py:13
  (14 other events, 8.4 us)
where the time goes:
time: 156 us; the launch traced here: 155 us
  waiting for transfers between devices  70.3 us (45%)
  starting transfers between devices  63.5 us (41%)
  matrix products  11.3 us (7%)
  local copies, waits for them, and re-layouts  8.01 us (5%)
    ppermute x16, waiting for transfers between devices, from_behind(): return lax.ppermute(block, axis, route)  53.8 us
    ppermute x16, starting transfers between devices, from_behind(): return lax.ppermute(block, axis, route)  46.4 us
    dot_general x16, matrix products, apply_block(): jnp.einsum('bij,bsj->bsi', matrix, vectors, precision=lax.Precision.HIGHEST)  8.26 us
    all_to_all x1, starting transfers between devices, body(): lax.all_to_all(send_codes, 'layer', split_axis=0, concat_axis=0, tiled=True)  7.25 us
    all_to_all x1, waiting for transfers between devices, body(): lax.all_to_all(send_tiles, 'layer', split_axis=0, concat_axis=0, tiled=True)  5.94 us
    all_to_all x1, waiting for transfers between devices, body(): lax.all_to_all(send_codes, 'layer', split_axis=0, concat_axis=0, tiled=True)  4.95 us
    all_to_all x1, waiting for transfers between devices, body(): lax.all_to_all(lax.all_to_all(send_tiles, 'layer', split_axis=0, concat_a...  3.66 us
    all_to_all x1, starting transfers between devices, body(): lax.all_to_all(send_tiles, 'layer', split_axis=0, concat_axis=0, tiled=True)  3.34 us
  transfers between devices with their start and end apart: 20, of which 20 were waited for; matrix products, arithmetic and copies ran while one was open for 3% of the time, Pallas kernels for 0%

commit v1 on v0

v1 whole, which is shorter than its diff:
```python
import functools

import jax
import jax.numpy as jnp
from jax import lax
from jax.experimental import pallas as pl
from jax.experimental.pallas import tpu as pltpu
from jax.sharding import PartitionSpec as P

MESH = pl.DeviceIdType.MESH
F32 = jnp.float32
BF16 = jnp.bfloat16
GROUP = 32


def nt(vectors, matrix):
    return lax.dot_general(vectors, matrix, (((1,), (1,)), ((), ())), preferred_element_type=F32)


def split(values):
    high = values.astype(BF16)
    return high, (values - high.astype(F32)).astype(BF16)


def apply_wide(values, matrix):
    high, low = split(values)
    both = nt(jnp.concatenate([high.astype(F32), low.astype(F32)], axis=0).astype(BF16), matrix)
    rows = values.shape[0]
    return both[:rows] + both[rows:]


def kernel(
    layers, lateral,
    inv, tiles, dest, code, out,
    send, recv, chalf, ohalf, far, comp_hi, comp_lo, acc, give, po, cin, oin, fout,
    load_sem, send_sem, recv_sem, far_send, far_recv, po_send, po_recv, c_send, c_recv, o_send, o_recv,
):
    layer = lax.axis_index("layer")
    lat = lax.axis_index("lat")
    devices = layers * lateral
    me = layer * lateral + lat
    x = lax.rem(layer, 2)
    group = layer // 2
    groups = layers // 2
    step = 2 * x - 1
    place = jnp.where(x == 1, group, groups - 1 - group)
    blocks, size, r = chalf.shape
    src = acc.shape[1]
    count = tiles.shape[0]
    mine = pl.multiple_of((1 - x) * r, r)
    other = pl.multiple_of(x * r, r)

    loads = [
        pltpu.make_async_copy(inv.at[0, :, :, pl.ds(mine, r)], chalf, load_sem.at[0]),
        pltpu.make_async_copy(inv.at[0, :, :, pl.ds(other, r)], ohalf, load_sem.at[1]),
    ]
    for load in loads:
        load.start()

    barrier = pltpu.get_barrier_semaphore()

    @pl.loop(1, devices)
    def _(i):
        to = lax.rem(me + i, devices)
        pl.semaphore_signal(
            barrier, inc=1, device_id=(to // lateral, lax.rem(to, lateral)), device_id_type=MESH
        )

    row_t = lax.broadcasted_iota(jnp.int32, (count, count), 0)
    col_t = lax.broadcasted_iota(jnp.int32, (count, count), 1)
    named = jnp.broadcast_to(dest[...], (count, count))
    target = jnp.sum(jnp.where(row_t == col_t, named, 0), axis=0, keepdims=True)
    order = jnp.sum(
        jnp.where((named == target) & (row_t < col_t), 1, 0), axis=0, keepdims=True
    )
    codes = jnp.broadcast_to(code[...], (count, count)) + 1
    code_col = jnp.sum(jnp.where(row_t == col_t, codes, 0), axis=1, keepdims=True)
    half = r // 2
    parts = [
        tiles[:, :half],
        tiles[:, half:],
        jnp.broadcast_to(code_col, (count, half)).astype(F32).astype(BF16),
    ]
    shape_w = (GROUP * 8, count)
    row_w = lax.broadcasted_iota(jnp.int32, shape_w, 0)
    q_w = row_w % 8
    slot_w = jnp.where(q_w < 4, q_w // 2, q_w - 4)
    kind_w = jnp.where(q_w < 4, q_w % 2, jnp.where(q_w < 6, 2, 3))

    def pack(chunk):
        hit = (target == chunk * GROUP + row_w // 8) & (order == slot_w)
        message = jnp.zeros((GROUP * 8, half), F32)
        for kind, part in enumerate(parts):
            picks = jnp.where(hit & (kind_w == kind), 1.0, 0.0).astype(BF16)
            message = message + jnp.dot(picks, part, preferred_element_type=F32)
        send[pl.ds(chunk * GROUP, GROUP)] = message.reshape(GROUP, 8, half).astype(BF16)

    if devices == GROUP:
        pack(0)
    else:
        pl.loop(0, devices // GROUP)(pack)
    recv[me] = send[me]

    pl.semaphore_wait(barrier, devices - 1)

    @pl.loop(1, devices)
    def _(i):
        to = lax.rem(me + i, devices)
        pltpu.make_async_remote_copy(
            src_ref=send.at[to],
            dst_ref=recv.at[me],
            send_sem=send_sem,
            recv_sem=recv_sem,
            device_id=(to // lateral, lax.rem(to, lateral)),
            device_id_type=MESH,
        ).start()

    partner = (layer - step, lat)
    far_copy = pltpu.make_async_remote_copy(
        src_ref=inv.at[0, :, pl.ds(mine, r), pl.ds(other, r)],
        dst_ref=far,
        send_sem=far_send,
        recv_sem=far_recv,
        device_id=partner,
        device_id_type=MESH,
    )
    far_copy.start()

    for load in loads:
        load.wait()
    far_copy.wait_recv()
    for b in range(blocks):
        product = jnp.dot(
            chalf[b, pl.ds(other, r), :], far[b], preferred_element_type=F32
        )
        high, low = split(product)
        comp_hi[b] = high
        comp_lo[b] = low

    rest = pl.ds(0, devices - 1)
    pltpu.make_async_copy(recv.at[rest], recv.at[rest], recv_sem).wait()

    shape_u = (GROUP, 8, half)
    q_u = lax.broadcasted_iota(jnp.int32, shape_u, 1)
    lane = lax.broadcasted_iota(jnp.int32, shape_u, 2)
    s_of, half_of, plane_of, block_of = lane % 8, (lane // 8) % 2, (lane // 16) % 2, lane // 32
    wanted = (((s_of * 2 + plane_of) * blocks + block_of) + 1).astype(F32)
    usable = (q_u < 4) & (q_u % 2 == half_of) & (lane < 64)

    def unpack(chunk):
        got = recv[pl.ds(chunk * GROUP, GROUP)].astype(F32)
        named_code = jnp.where(q_u < 2, got[:, 4:5, :], got[:, 5:6, :])
        table = jnp.where(usable & (named_code == wanted), 1.0, 0.0)
        return lax.dot_general(
            table.reshape(GROUP * 8, half).astype(BF16),
            got.reshape(GROUP * 8, half).astype(BF16),
            (((0,), (0,)), ((), ())),
            preferred_element_type=F32,
        )

    if devices == GROUP:
        field = unpack(0)
    else:
        field = lax.fori_loop(
            0, devices // GROUP, lambda i, total: total + unpack(i), jnp.zeros((half, half), F32)
        )

    owned = []
    upper = x == 1
    for b in range(blocks):
        rows = [field[32 * b + 8 * k : 32 * b + 8 * k + 8] for k in range(4)]
        top = jnp.concatenate(rows[:2], axis=1)
        bottom = jnp.concatenate(rows[2:], axis=1)
        own = jnp.where(upper, top, bottom).astype(BF16)
        away = jnp.where(upper, bottom, top).astype(BF16)
        local = nt(own, chalf[b]) + nt(away, ohalf[b])
        acc[b] = local
        give[b] = jnp.where(upper, local[:, :r], local[:, r:])
        owned.append(jnp.where(upper, local[:, r:], local[:, :r]))

    po_copy = pltpu.make_async_remote_copy(
        src_ref=give, dst_ref=po, send_sem=po_send, recv_sem=po_recv,
        device_id=partner, device_id_type=MESH,
    )
    po_copy.start()
    po_copy.wait_recv()
    for b in range(blocks):
        fout[b] = apply_wide(po[b], chalf[b, pl.ds(other, r), :]) + owned[b]

    onward = layer + 2 * step
    c_copy = pltpu.make_async_remote_copy(
        src_ref=fout, dst_ref=cin, send_sem=c_send, recv_sem=c_recv,
        device_id=(onward, lat), device_id_type=MESH,
    )
    o_copy = pltpu.make_async_remote_copy(
        src_ref=fout, dst_ref=oin, send_sem=o_send, recv_sem=o_recv,
        device_id=(onward - step, lat), device_id_type=MESH,
    )
    last = place == groups - 1
    first = place == 0

    def forward():
        @pl.when(jnp.logical_not(last))
        def _():
            c_copy.start()
            o_copy.start()

    def chain():
        @pl.when(first)
        def _():
            forward()
            for b in range(blocks):
                acc[b] = acc[b] + nt(po[b].astype(BF16), chalf[b])

        @pl.when(jnp.logical_not(first))
        def _():
            c_copy.wait_recv()

            @pl.when(jnp.logical_not(last))
            def _():
                for b in range(blocks):
                    state = cin[b]
                    fout[b] = (
                        fout[b]
                        + apply_wide(state, comp_hi[b])
                        + nt(state.astype(BF16), comp_lo[b])
                    )

            forward()
            for b in range(blocks):
                trace = apply_wide(cin[b], far[b]) + po[b]
                acc[b] = acc[b] + nt(trace.astype(BF16), chalf[b])

    def opposite():
        @pl.when(jnp.logical_not(last))
        def _():
            o_copy.wait_recv()
            for b in range(blocks):
                acc[b] = acc[b] + nt(oin[b].astype(BF16), ohalf[b])

    early = 2 * place < groups

    @pl.when(early)
    def _():
        chain()
        opposite()

    @pl.when(jnp.logical_not(early))
    def _():
        opposite()
        chain()

    for b in range(blocks):
        out[0, b] = acc[b]

    @pl.when(jnp.logical_not(last))
    def _():
        c_copy.wait_send()
        o_copy.wait_send()

    po_copy.wait_send()
    far_copy.wait_send()
    pltpu.make_async_copy(send.at[rest], send.at[rest], send_sem).wait()


def body(layers, lateral, inverse, tiles, tile_dest, tile_code):
    devices = layers * lateral
    _, blocks, size, _ = inverse.shape
    r = tiles.shape[1]
    src = 8
    dma = pltpu.SemaphoreType.DMA
    small = (blocks, src, r)
    vmem = pl.BlockSpec(memory_space=pltpu.VMEM)
    return pl.pallas_call(
        functools.partial(kernel, layers, lateral),
        out_shape=jax.ShapeDtypeStruct((1, blocks, src, size), F32),
        in_specs=[pl.BlockSpec(memory_space=pl.ANY), vmem, vmem, vmem],
        out_specs=vmem,
        scratch_shapes=[
            pltpu.VMEM((devices, 8, r // 2), BF16),
            pltpu.VMEM((devices, 8, r // 2), BF16),
            pltpu.VMEM((blocks, size, r), BF16),
            pltpu.VMEM((blocks, size, r), BF16),
            pltpu.VMEM((blocks, r, r), BF16),
            pltpu.VMEM((blocks, r, r), BF16),
            pltpu.VMEM((blocks, r, r), BF16),
            pltpu.VMEM((blocks, src, size), F32),
            pltpu.VMEM(small, F32),
            pltpu.VMEM(small, F32),
            pltpu.VMEM(small, F32),
            pltpu.VMEM(small, F32),
            pltpu.VMEM(small, F32),
            dma((2,)),
        ]
        + [dma] * 10,
        compiler_params=pltpu.CompilerParams(
            collective_id=0, has_side_effects=True, vmem_limit_bytes=48 * 1024 * 1024
        ),
        name="sweep",
    )(inverse, tiles, tile_dest, tile_code.reshape(1, -1))


def solution(mesh):
    in_specs = (
        P("layer", "lat", None, None),
        P(("layer", "lat"), None),
        P(("layer", "lat"), None),
        P(("layer", "lat")),
    )
    out_specs = P("layer", "lat", None, None)
    return jax.shard_map(
        functools.partial(body, mesh.shape["layer"], mesh.shape["lat"]),
        mesh=mesh, in_specs=in_specs, out_specs=out_specs, check_vma=False,
    )
```

time: 156 us -> 31.1 us (0.20)
  waiting for transfers between devices: 70.3 us -> 0 us
  starting transfers between devices: 63.5 us -> 0 us
  Pallas kernels: 0 us -> 27.7 us
  matrix products: 11.3 us -> 0 us
  local copies, waits for them, and re-layouts: 8.01 us -> 3.15 us
    ppermute x16 -> x0, waiting for transfers between devices: 53.8 us -> none  [from_behind(): return lax.ppermute(block, axis, route)]
    ppermute x16 -> x0, starting transfers between devices: 46.4 us -> none  [from_behind(): return lax.ppermute(block, axis, route)]
    pallas_call x0 -> x1, Pallas kernels: none -> 27.7 us  [body(): pl.pallas_call(functools.partial(kernel, layers, lateral), out_shape=jax....]
    all_to_all x4 -> x0, starting transfers between devices: 17.1 us -> none  [the longest x1 7.25 us: body(): lax.all_to_all(send_codes, 'layer', split_axis=0, concat_axis=0, tiled=True)]
    all_to_all x4 -> x0, waiting for transfers between devices: 16.5 us -> none  [the longest x1 5.94 us: body(): lax.all_to_all(send_tiles, 'layer', split_axis=0, concat_axis=0, tiled=True)]
    dot_general x20 -> x0, matrix products: 11.3 us -> none  [the longest x16 8.26 us: apply_block(): jnp.einsum('bij,bsj->bsi', matrix, vectors, precision=lax.Precision.HIGHEST)]
    unnamed x4 -> x10, local copies, waits for them, and re-layouts: 0.66 us -> 3.15 us
    scatter x2 -> x0, local copies, waits for them, and re-layouts: 1.72 us -> none  [the longest x1 0.91 us: body(): jnp.zeros((devices * CAP, trace_len), jnp.bfloat16).at[slot_at].set(tiles)]
  transfers between devices with their start and end apart: 20 -> 0, of which waited for: 20 -> 0; matrix products, arithmetic and copies ran while one was open for 3% -> 0% of each run, Pallas kernels for 0% -> 0%
where the time goes in v1:
time: 31.1 us; the launch traced here: 30.9 us
  Pallas kernels  27.7 us (89%)
  local copies, waits for them, and re-layouts  3.15 us (10%)
    pallas_call x1, Pallas kernels, body(): pl.pallas_call(functools.partial(kernel, layers, lateral), out_shape=jax....  27.7 us
    unnamed x10, local copies, waits for them, and re-layouts  3.15 us

profile of v1, /device:TPU:0, one launch (start us, length us, event | category | flops | bytes accessed | tf_op | source)
XLA Modules:
  0.0 30.9 jit_solution(2394537012932194611)
XLA Ops:
  0.0 0.0 copy-start.3
  0.0 0.0 copy-start.1
  0.0 0.7 %copy-done.3 = s32[32,1]{0,1:T(1,128)S(1)} copy-done((s32[32,1]{0,1:T(1,128)S(1)}, s32[32,1]{0,1:T(1,128)}, u32[]{:S(2)}) %copy-start.3) | copy-done | bytes 152
  0.7 0.0 copy-start.2
  0.7 0.1 copy.5.dest
  0.7 0.0 copy-done.1
  0.7 0.6 %copy-done.2 = s32[32]{0:T(128)S(1)} copy-done((s32[32]{0:T(128)S(1)}, s32[32]{0:T(128)}, u32[]{:S(2)}) %copy-start.2) | copy-done | bytes 152
  1.3 0.0 copy-start
  1.3 1.2 %copy-done = bf16[1,2,512,512]{3,2,1,0:T(8,128)(2,1)S(1)} copy-done((bf16[1,2,512,512]{3,2,1,0:T(8,128)(2,1)S(1)}, bf16[1,2,512,512]{3,2,1,0:T(8,128)(2,1)}, u32[]{:S(2)}) %copy-start) | copy-done | bytes 1048600
  2.5 27.7 %sweep.1 = f32[1,2,8,512]{3,2,1,0:T(8,128)S(1)} custom-call(bf16[1,2,512,512]{3,2,1,0:T(8,128)(2,1)S(1)} %copy-done, bf16[32,256]{1,0:T(8,128)(2,1)S(1)} %copy-done.1, s32[32,1]{1,0:T(8,128)S(1)} %copy.5.dest, s32[1,32]{1,0:T(1,128)S(1)} %bitcast.1), custom_call_target="tpu_custom_call" | custom-call | tf_op jit(solution)/shard_map/sweep/pallas_call | solution.py:274
  30.3 0.6 %copy.7 = f32[1,2,8,512]{3,2,1,0:T(8,128)} copy(f32[1,2,8,512]{3,2,1,0:T(8,128)S(1)} %sweep.1) | data formatting | bytes 65536
Async XLA Ops:
  0.0 0.7 %copy-start.3 = (s32[32,1]{0,1:T(1,128)S(1)}, s32[32,1]{0,1:T(1,128)}, u32[]{:S(2)}) copy-start(s32[32,1]{0,1:T(1,128)} %param.6) | copy-start | bytes 388
  0.0 0.7 %copy-start.1 = (bf16[32,256]{1,0:T(8,128)(2,1)S(1)}, bf16[32,256]{1,0:T(8,128)(2,1)}, u32[]{:S(2)}) copy-start(bf16[32,256]{1,0:T(8,128)(2,1)} %tiles.1) | copy-start | bytes 49156
  0.7 0.7 %copy-start.2 = (s32[32]{0:T(128)S(1)}, s32[32]{0:T(128)}, u32[]{:S(2)}) copy-start(s32[32]{0:T(128)} %param.7) | copy-start | bytes 388
  1.3 1.2 %copy-start = (bf16[1,2,512,512]{3,2,1,0:T(8,128)(2,1)S(1)}, bf16[1,2,512,512]{3,2,1,0:T(8,128)(2,1)}, u32[]{:S(2)}) copy-start(bf16[1,2,512,512]{3,2,1,0:T(8,128)(2,1)} %inv.1) | copy-start | bytes 3145732

commit v2 on v1

--- a/solution.py
+++ b/solution.py
@@ -17,23 +17,11 @@
     return lax.dot_general(vectors, matrix, (((1,), (1,)), ((), ())), preferred_element_type=F32)
 
 
-def split(values):
-    high = values.astype(BF16)
-    return high, (values - high.astype(F32)).astype(BF16)
-
-
-def apply_wide(values, matrix):
-    high, low = split(values)
-    both = nt(jnp.concatenate([high.astype(F32), low.astype(F32)], axis=0).astype(BF16), matrix)
-    rows = values.shape[0]
-    return both[:rows] + both[rows:]
-
-
 def kernel(
     layers, lateral,
-    inv, tiles, dest, code, out,
-    send, recv, chalf, ohalf, far, comp_hi, comp_lo, acc, give, po, cin, oin, fout,
-    load_sem, send_sem, recv_sem, far_send, far_recv, po_send, po_recv, c_send, c_recv, o_send, o_recv,
+    inv, tiles_in, dest_in, code_in, out,
+    tiles, dest, code, send, recv, chalf, ohalf, far, comp, acc, base, give, po, cin, oin, fout,
+    small_sem, load_sem, send_sem, recv_sem, far_send, far_recv, po_send, po_recv, c_send, c_recv, o_send, o_recv,
 ):
     layer = lax.axis_index("layer")
     lat = lax.axis_index("lat")
@@ -50,12 +38,16 @@
     mine = pl.multiple_of((1 - x) * r, r)
     other = pl.multiple_of(x * r, r)
 
+    smalls = [
+        pltpu.make_async_copy(source, target, small_sem.at[i])
+        for i, (source, target) in enumerate(((tiles_in, tiles), (dest_in, dest), (code_in, code)))
+    ]
+    for load in smalls:
+        load.start()
     loads = [
         pltpu.make_async_copy(inv.at[0, :, :, pl.ds(mine, r)], chalf, load_sem.at[0]),
         pltpu.make_async_copy(inv.at[0, :, :, pl.ds(other, r)], ohalf, load_sem.at[1]),
     ]
-    for load in loads:
-        load.start()
 
     barrier = pltpu.get_barrier_semaphore()
 
@@ -66,10 +58,16 @@
             barrier, inc=1, device_id=(to // lateral, lax.rem(to, lateral)), device_id_type=MESH
         )
 
+    for load in loads:
+        load.start()
+    for load in smalls:
+        load.wait()
+
     row_t = lax.broadcasted_iota(jnp.int32, (count, count), 0)
     col_t = lax.broadcasted_iota(jnp.int32, (count, count), 1)
-    named = jnp.broadcast_to(dest[...], (count, count))
-    target = jnp.sum(jnp.where(row_t == col_t, named, 0), axis=0, keepdims=True)
+    target = dest[...]
+    across = jnp.broadcast_to(target, (count, count))
+    named = jnp.sum(jnp.where(row_t == col_t, across, 0), axis=1, keepdims=True)
     order = jnp.sum(
         jnp.where((named == target) & (row_t < col_t), 1, 0), axis=0, keepdims=True
     )
@@ -128,14 +126,6 @@
 
     for load in loads:
         load.wait()
-    far_copy.wait_recv()
-    for b in range(blocks):
-        product = jnp.dot(
-            chalf[b, pl.ds(other, r), :], far[b], preferred_element_type=F32
-        )
-        high, low = split(product)
-        comp_hi[b] = high
-        comp_lo[b] = low
 
     rest = pl.ds(0, devices - 1)
     pltpu.make_async_copy(recv.at[rest], recv.at[rest], recv_sem).wait()
@@ -175,7 +165,7 @@
         away = jnp.where(upper, bottom, top).astype(BF16)
         local = nt(own, chalf[b]) + nt(away, ohalf[b])
         acc[b] = local
-        give[b] = jnp.where(upper, local[:, :r], local[:, r:])
+        give[b] = jnp.where(upper, local[:, :r], local[:, r:]).astype(BF16)
         owned.append(jnp.where(upper, local[:, r:], local[:, :r]))
 
     po_copy = pltpu.make_async_remote_copy(
@@ -185,7 +175,9 @@
     po_copy.start()
     po_copy.wait_recv()
     for b in range(blocks):
-        fout[b] = apply_wide(po[b], chalf[b, pl.ds(other, r), :]) + owned[b]
+        total = nt(po[b], chalf[b, pl.ds(other, r), :]) + owned[b]
+        base[b] = total
+        fout[b] = total.astype(BF16)
 
     onward = layer + 2 * step
     c_copy = pltpu.make_async_remote_copy(
@@ -205,12 +197,24 @@
             c_copy.start()
             o_copy.start()
 
+    @pl.when(first)
+    def _():
+        forward()
+
+    far_copy.wait_recv()
+
+    @pl.when(jnp.logical_not(first | last))
+    def _():
+        for b in range(blocks):
+            comp[b] = jnp.dot(
+                chalf[b, pl.ds(other, r), :], far[b], preferred_element_type=F32
+            ).astype(BF16)
+
     def chain():
         @pl.when(first)
         def _():
-            forward()
             for b in range(blocks):
-                acc[b] = acc[b] + nt(po[b].astype(BF16), chalf[b])
+                acc[b] = acc[b] + nt(po[b], chalf[b])
 
         @pl.when(jnp.logical_not(first))
         def _():
@@ -219,16 +223,11 @@
             @pl.when(jnp.logical_not(last))
             def _():
                 for b in range(blocks):
-                    state = cin[b]
-                    fout[b] = (
-                        fout[b]
-                        + apply_wide(state, comp_hi[b])
-                        + nt(state.astype(BF16), comp_lo[b])
-                    )
+                    fout[b] = (base[b] + nt(cin[b], comp[b])).astype(BF16)
 
             forward()
             for b in range(blocks):
-                trace = apply_wide(cin[b], far[b]) + po[b]
+                trace = nt(cin[b], far[b]) + po[b].astype(F32)
                 acc[b] = acc[b] + nt(trace.astype(BF16), chalf[b])
 
     def opposite():
@@ -236,7 +235,7 @@
         def _():
             o_copy.wait_recv()
             for b in range(blocks):
-                acc[b] = acc[b] + nt(oin[b].astype(BF16), ohalf[b])
+                acc[b] = acc[b] + nt(oin[b], ohalf[b])
 
     early = 2 * place < groups
 
@@ -274,22 +273,26 @@
     return pl.pallas_call(
         functools.partial(kernel, layers, lateral),
         out_shape=jax.ShapeDtypeStruct((1, blocks, src, size), F32),
-        in_specs=[pl.BlockSpec(memory_space=pl.ANY), vmem, vmem, vmem],
+        in_specs=[pl.BlockSpec(memory_space=pltpu.HBM)] * 4,
         out_specs=vmem,
         scratch_shapes=[
+            pltpu.VMEM(tiles.shape, BF16),
+            pltpu.VMEM((1, tiles.shape[0]), jnp.int32),
+            pltpu.VMEM((1, tiles.shape[0]), jnp.int32),
             pltpu.VMEM((devices, 8, r // 2), BF16),
             pltpu.VMEM((devices, 8, r // 2), BF16),
             pltpu.VMEM((blocks, size, r), BF16),
             pltpu.VMEM((blocks, size, r), BF16),
             pltpu.VMEM((blocks, r, r), BF16),
             pltpu.VMEM((blocks, r, r), BF16),
-            pltpu.VMEM((blocks, r, r), BF16),
             pltpu.VMEM((blocks, src, size), F32),
             pltpu.VMEM(small, F32),
-            pltpu.VMEM(small, F32),
-            pltpu.VMEM(small, F32),
-            pltpu.VMEM(small, F32),
-            pltpu.VMEM(small, F32),
+            pltpu.VMEM(small, BF16),
+            pltpu.VMEM(small, BF16),
+            pltpu.VMEM(small, BF16),
+            pltpu.VMEM(small, BF16),
+            pltpu.VMEM(small, BF16),
+            dma((3,)),
             dma((2,)),
         ]
         + [dma] * 10,
@@ -297,7 +300,12 @@
             collective_id=0, has_side_effects=True, vmem_limit_bytes=48 * 1024 * 1024
         ),
         name="sweep",
-    )(inverse, tiles, tile_dest, tile_code.reshape(1, -1))
+    )(
+        *(
+            pltpu.with_memory_space_constraint(array, pltpu.HBM)
+            for array in (inverse, tiles, tile_dest.reshape(1, -1), tile_code.reshape(1, -1))
+        )
+    )
 
 
 def solution(mesh):

time: 31.1 us -> 24.5 us (0.79)
  Pallas kernels: 27.7 us -> 23.7 us
  local copies, waits for them, and re-layouts: 3.15 us -> 0.62 us
    pallas_call x1, Pallas kernels: 27.7 us -> 23.7 us  [body(): pl.pallas_call(functools.partial(kernel, layers, lateral), out_shape=jax....]
    unnamed x10 -> x1, local copies, waits for them, and re-layouts: 3.15 us -> 0.62 us
where the time goes in v2:
time: 24.5 us; the launch traced here: 24.3 us
  Pallas kernels  23.7 us (97%)
  local copies, waits for them, and re-layouts  0.62 us (3%)
    pallas_call x1, Pallas kernels, body(): pl.pallas_call(functools.partial(kernel, layers, lateral), out_shape=jax....  23.7 us
    unnamed x1, local copies, waits for them, and re-layouts  0.62 us

profile of v2, /device:TPU:0, one launch (start us, length us, event | category | flops | bytes accessed | tf_op | source)
XLA Modules:
  0.0 24.3 jit_solution(8302061995948245732)
XLA Ops:
  0.0 23.7 %sweep.1 = f32[1,2,8,512]{3,2,1,0:T(8,128)S(1)} custom-call(bf16[1,2,512,512]{3,2,1,0:T(8,128)(2,1)} %inv.1, bf16[32,256]{1,0:T(8,128)(2,1)} %tiles_in.1, s32[1,32]{1,0:T(1,128)} %bitcast.2, s32[1,32]{1,0:T(1,128)} %bitcast.3), custom_call_target="tpu_custom_call" | custom-call | tf_op jit(solution)/shard_map/sweep/pallas_call | solution.py:273
  23.7 0.6 %copy.6 = f32[1,2,8,512]{3,2,1,0:T(8,128)} copy(f32[1,2,8,512]{3,2,1,0:T(8,128)S(1)} %sweep.1) | data formatting | bytes 65536

commit v3 on v2

--- a/solution.py
+++ b/solution.py
@@ -38,6 +38,38 @@
     mine = pl.multiple_of((1 - x) * r, r)
     other = pl.multiple_of(x * r, r)
 
+    barrier = pltpu.get_barrier_semaphore()
+
+    def wrap(index, length):
+        return jnp.where(index >= length, index - length, index)
+
+    def others(visit):
+        def visit_layer(i):
+            to = jnp.where(layer < layers // 2, layers - 1 - i, i)
+
+            def visit_lat(across):
+                visit(to, wrap(lat + across, lateral))
+
+            for across in range(1, lateral):
+                visit_lat(across)
+
+            @pl.when(to != layer)
+            def _():
+                visit_lat(0)
+
+        if devices == GROUP:
+            for i in range(layers):
+                visit_layer(i)
+        else:
+            pl.loop(0, layers)(visit_layer)
+
+    def greet(to_layer, to_lat):
+        pl.semaphore_signal(
+            barrier, inc=1, device_id=(to_layer, to_lat), device_id_type=MESH
+        )
+
+    others(greet)
+
     smalls = [
         pltpu.make_async_copy(source, target, small_sem.at[i])
         for i, (source, target) in enumerate(((tiles_in, tiles), (dest_in, dest), (code_in, code)))
@@ -48,15 +80,6 @@
         pltpu.make_async_copy(inv.at[0, :, :, pl.ds(mine, r)], chalf, load_sem.at[0]),
         pltpu.make_async_copy(inv.at[0, :, :, pl.ds(other, r)], ohalf, load_sem.at[1]),
     ]
-
-    barrier = pltpu.get_barrier_semaphore()
-
-    @pl.loop(1, devices)
-    def _(i):
-        to = lax.rem(me + i, devices)
-        pl.semaphore_signal(
-            barrier, inc=1, device_id=(to // lateral, lax.rem(to, lateral)), device_id_type=MESH
-        )
 
     for load in loads:
         load.start()
@@ -101,17 +124,17 @@
 
     pl.semaphore_wait(barrier, devices - 1)
 
-    @pl.loop(1, devices)
-    def _(i):
-        to = lax.rem(me + i, devices)
+    def route(to_layer, to_lat):
         pltpu.make_async_remote_copy(
-            src_ref=send.at[to],
+            src_ref=send.at[to_layer * lateral + to_lat],
             dst_ref=recv.at[me],
             send_sem=send_sem,
             recv_sem=recv_sem,
-            device_id=(to // lateral, lax.rem(to, lateral)),
+            device_id=(to_layer, to_lat),
             device_id_type=MESH,
         ).start()
+
+    others(route)
 
     partner = (layer - step, lat)
     far_copy = pltpu.make_async_remote_copy(

time: 24.5 us -> 24.1 us (0.984)
  Pallas kernels: 23.7 us -> 23.3 us
    pallas_call x1, Pallas kernels: 23.7 us -> 23.3 us  [body(): pl.pallas_call(functools.partial(kernel, layers, lateral), out_shape=jax....]
where the time goes in v3:
time: 24.1 us; the launch traced here: 23.9 us
  Pallas kernels  23.3 us (97%)
  local copies, waits for them, and re-layouts  0.62 us (3%)
    pallas_call x1, Pallas kernels, body(): pl.pallas_call(functools.partial(kernel, layers, lateral), out_shape=jax....  23.3 us
    unnamed x1, local copies, waits for them, and re-layouts  0.62 us

profile of v3, /device:TPU:0, one launch (start us, length us, event | category | flops | bytes accessed | tf_op | source)
XLA Modules:
  0.0 23.9 jit_solution(65349127086558759)
XLA Ops:
  0.0 23.3 %sweep.1 = f32[1,2,8,512]{3,2,1,0:T(8,128)S(1)} custom-call(bf16[1,2,512,512]{3,2,1,0:T(8,128)(2,1)} %inv.1, bf16[32,256]{1,0:T(8,128)(2,1)} %tiles_in.1, s32[1,32]{1,0:T(1,128)} %bitcast.2, s32[1,32]{1,0:T(1,128)} %bitcast.3), custom_call_target="tpu_custom_call" | custom-call | tf_op jit(solution)/shard_map/sweep/pallas_call | solution.py:296
  23.3 0.6 %copy.6 = f32[1,2,8,512]{3,2,1,0:T(8,128)} copy(f32[1,2,8,512]{3,2,1,0:T(8,128)S(1)} %sweep.1) | data formatting | bytes 65536

commit v4 on v3

--- a/solution.py
+++ b/solution.py
@@ -124,6 +124,17 @@
 
     pl.semaphore_wait(barrier, devices - 1)
 
+    partner = (layer - step, lat)
+    far_copy = pltpu.make_async_remote_copy(
+        src_ref=inv.at[0, :, pl.ds(mine, r), pl.ds(other, r)],
+        dst_ref=far,
+        send_sem=far_send,
+        recv_sem=far_recv,
+        device_id=partner,
+        device_id_type=MESH,
+    )
+    far_copy.start()
+
     def route(to_layer, to_lat):
         pltpu.make_async_remote_copy(
             src_ref=send.at[to_layer * lateral + to_lat],
@@ -135,17 +146,6 @@
         ).start()
 
     others(route)
-
-    partner = (layer - step, lat)
-    far_copy = pltpu.make_async_remote_copy(
-        src_ref=inv.at[0, :, pl.ds(mine, r), pl.ds(other, r)],
-        dst_ref=far,
-        send_sem=far_send,
-        recv_sem=far_recv,
-        device_id=partner,
-        device_id_type=MESH,
-    )
-    far_copy.start()
 
     for load in loads:
         load.wait()

time: 24.1 us -> 27.4 us (1.14)
  Pallas kernels: 23.3 us -> 26.5 us
    pallas_call x1, Pallas kernels: 23.3 us -> 26.5 us  [body(): pl.pallas_call(functools.partial(kernel, layers, lateral), out_shape=jax....]
where the time goes in v4:
time: 27.4 us; the launch traced here: 27.1 us
  Pallas kernels  26.5 us (97%)
  local copies, waits for them, and re-layouts  0.62 us (2%)
    pallas_call x1, Pallas kernels, body(): pl.pallas_call(functools.partial(kernel, layers, lateral), out_shape=jax....  26.5 us
    unnamed x1, local copies, waits for them, and re-layouts  0.62 us

profile of v4, /device:TPU:0, one launch (start us, length us, event | category | flops | bytes accessed | tf_op | source)
XLA Modules:
  0.0 27.1 jit_solution(18271269150961908000)
XLA Ops:
  0.0 26.5 %sweep.1 = f32[1,2,8,512]{3,2,1,0:T(8,128)S(1)} custom-call(bf16[1,2,512,512]{3,2,1,0:T(8,128)(2,1)} %inv.1, bf16[32,256]{1,0:T(8,128)(2,1)} %tiles_in.1, s32[1,32]{1,0:T(1,128)} %bitcast.2, s32[1,32]{1,0:T(1,128)} %bitcast.3), custom_call_target="tpu_custom_call" | custom-call | tf_op jit(solution)/shard_map/sweep/pallas_call | solution.py:296
  26.5 0.6 %copy.6 = f32[1,2,8,512]{3,2,1,0:T(8,128)} copy(f32[1,2,8,512]{3,2,1,0:T(8,128)S(1)} %sweep.1) | data formatting | bytes 65536
